TPU v7x, 768 devices: a whole 4x8x12 slice. The times are simulated.
768 devices in a mesh: dp: 32 (over y, x), tensor: 24 (over z, core).
Axes of the slice: x: 4, y: 8, z: 12, core: 2. Of those that a mesh axis runs over, the one named last changes fastest.
Arguments:
- inputs: float32 [24576, 2048], P(('dp', 'tensor')), parts along dimension 0, may hold values from -6 to 6
- out_grad: float32 [24576, 2048], P(('dp', 'tensor')), parts along dimension 0, may hold values from -6 to 6
- pre_saved: bfloat16 [24576, 9216], P('dp', 'tensor'), parts along dimension 0, may hold values from -6 to 6
- w_in: bfloat16 [2048, 9216], P(None, 'tensor'), may hold values from -0.125 to 0.125
- w_out_t: bfloat16 [2048, 9216], P(None, 'tensor'), may hold values from -0.0625 to 0.0625
Outputs:
- input_grad: float32 [24576, 2048], P(('dp', 'tensor')), parts along dimension 0
- grad_w_in: bfloat16 [65536, 9216], P('dp', 'tensor'), parts along dimension 0
- grad_w_out_t: bfloat16 [65536, 9216], P('dp', 'tensor'), parts along dimension 0
There are 32 independent parts, one for each index of `dp`. A program takes and returns all parts, laid end to end along the dimension named above; an argument that names none is the same for every part. Nothing has to cross between parts.
All inputs are finite; a program needn't handle non-finite values.
Results may differ from a plain program's by a relative error of at most 0.02.
Values may be sent and summed in bfloat16 or wider, within the bound.
A program may use at most 64 MiB of HBM per device.

v0:
```python
import jax
import jax.numpy as jnp
from jax import lax
from jax.sharding import PartitionSpec as P


def contract_rows(left, right):
    return lax.dot_general(
        left, right, (((0,), (0,)), ((), ())), preferred_element_type=jnp.float32
    )


def contract_cols(left, right):
    return lax.dot_general(
        left, right, (((1,), (1,)), ((), ())), preferred_element_type=jnp.float32
    )


def row_block(rows_grad, rows_pre, w_out_t):
    activ = jnp.maximum(rows_pre, jnp.zeros_like(rows_pre))
    back = jnp.dot(rows_grad, w_out_t, preferred_element_type=jnp.float32)
    hid_grad = jnp.where(rows_pre > 0.0, back, 0.0).astype(jnp.bfloat16)
    return (hid_grad, activ)


def on_device(inputs, out_grad, pre_saved, w_in, w_out_t):
    inputs_bf = inputs.astype(jnp.bfloat16)
    grad_bf = out_grad.astype(jnp.bfloat16)
    all_in, all_grad = (
        lax.all_gather(inputs_bf, "tensor", axis=0, tiled=True),
        lax.all_gather(grad_bf, "tensor", axis=0, tiled=True),
    )
    hid_grad, activ = row_block(all_grad, pre_saved, w_out_t)
    sum_out = contract_rows(all_grad, activ)
    sum_in = contract_rows(all_in, hid_grad)
    input_grad = lax.psum_scatter(
        contract_cols(hid_grad, w_in).astype(jnp.bfloat16),
        "tensor",
        scatter_dimension=0,
        tiled=True,
    ).astype(jnp.float32)
    return (input_grad, sum_in.astype(jnp.bfloat16), sum_out.astype(jnp.bfloat16))


def solution(mesh):
    in_specs = (
        P(("dp", "tensor"), None),
        P(("dp", "tensor"), None),
        P("dp", "tensor"),
        P(None, "tensor"),
        P(None, "tensor"),
    )
    out_specs = (P(("dp", "tensor"), None), P("dp", "tensor"), P("dp", "tensor"))
    return jax.shard_map(
        on_device, mesh=mesh, in_specs=in_specs, out_specs=out_specs, check_vma=False
    )
```

profile of v0, /device:TPU:1, one launch (start us, length us, event | category | flops | bytes accessed | tf_op | source)
XLA Modules:
  0.0 237.6 jit_solution(12747315270743539472)
XLA Ops:
  7.2 0.0 copy-start
  7.2 0.0 all-gather.3.cloned.1.call-start
  7.2 1.7 convert_element_type.27
  9.0 0.0 all-gather.3.cloned.1.call-update
  9.0 0.0 all-gather.5.cloned.1.call-start
  9.0 1.6 convert_element_type.31
  10.7 0.0 all-gather.5.cloned.1.call-update
  10.7 0.0 reduce-scatter.2.cloned.1.call-start
  10.7 69.1 %all-gather.3.cloned.1.call-done = bf16[768,2048]{1,0:T(8,128)(2,1)} async-done(((bf16[32,2048]{1,0:T(8,128)(2,1)}), bf16[768,2048]{1,0:T(8,128)(2,1)}) %all-gather.3.cloned.1.call-update) | async-done | bytes 3145744 | tf_op jit(solution)/shard_map/all_gather | solution.py:31
  79.8 4.3 %fusion.2 = bf16[768,384]{1,0:T(8,128)(2,1)S(1)} fusion(bf16[768,2048]{1,0:T(8,128)(2,1)} %all-gather.3.cloned.1.call-done, bf16[2048,384]{1,0:T(8,128)(2,1)} %param.9, bf16[768,384]{1,0:T(8,128)(2,1)} %param.7), kind=kOutput, calls=%fused_computation.6 | convolution fusion | flops 1208844288 | bytes 5898240 | tf_op jit(solution)/shard_map/dot_general | solution.py:21
  84.1 0.0 copy-start.1
  84.1 0.8 copy-done.1
  84.9 0.0 copy-done
  84.9 3.5 %convolution_convert_fusion = bf16[768,2048]{1,0:T(8,128)(2,1)} fusion(bf16[768,384]{1,0:T(8,128)(2,1)S(1)} %fusion.2, bf16[2048,384]{1,0:T(8,128)(2,1)S(1)} %copy-done), kind=kOutput, calls=%fused_computation | convolution fusion | flops 1209532416 | bytes 5308416 | tf_op jit(solution)/shard_map/dot_general | solution.py:14
  88.5 0.0 reduce-scatter.2.cloned.1.call-update
  88.5 52.2 %all-gather.5.cloned.1.call-done = bf16[768,2048]{1,0:T(8,128)(2,1)} async-done(((bf16[32,2048]{1,0:T(8,128)(2,1)}), bf16[768,2048]{1,0:T(8,128)(2,1)}) %all-gather.5.cloned.1.call-update) | async-done | bytes 3145744 | tf_op jit(solution)/shard_map/all_gather | solution.py:30
  140.7 3.5 %fusion = bf16[2048,384]{0,1:T(8,128)(2,1)S(1)} fusion(bf16[768,384]{1,0:T(8,128)(2,1)} %copy-done.1, bf16[768,2048]{1,0:T(8,128)(2,1)} %all-gather.5.cloned.1.call-done), kind=kOutput, calls=%fused_computation.3 | convolution fusion | flops 1208745984 | bytes 5308416 | tf_op jit(solution)/shard_map/dot_general | solution.py:8
  144.2 1.6 copy.8
  145.8 3.5 %fusion.1 = bf16[2048,384]{0,1:T(8,128)(2,1)S(1)} fusion(bf16[768,2048]{1,0:T(8,128)(2,1)} %all-gather.3.cloned.1.call-done, bf16[768,384]{1,0:T(8,128)(2,1)} %param.7), kind=kOutput, calls=%fused_computation.4 | convolution fusion | flops 1209040896 | bytes 5308416 | tf_op jit(solution)/shard_map/dot_general | solution.py:8
  149.3 1.6 copy.9
  150.8 78.6 %reduce-scatter.2.cloned.1.call-done = bf16[32,2048]{1,0:T(8,128)(2,1)} async-done(((bf16[768,2048]{1,0:T(8,128)(2,1)}), bf16[32,2048]{1,0:T(8,128)(2,1)}) %reduce-scatter.2.cloned.1.call-update) | async-done | bytes 131088 | tf_op jit(solution)/shard_map/reduce_scatter | solution.py:36
  229.4 1.6 convert_element_type.30
Async XLA Ops:
  7.2 77.8 %copy-start = (bf16[2048,384]{1,0:T(8,128)(2,1)S(1)}, bf16[2048,384]{1,0:T(8,128)(2,1)}, u32[]{:S(2)}) copy-start(bf16[2048,384]{1,0:T(8,128)(2,1)} %param.8) | copy-start | bytes 4718596
  7.2 72.7 %all-gather.3.cloned.1.call-start = ((), (), s32[]{:S(2)}) async-start(), calls=%async_computation.1 | async-start | bytes 3276800 | tf_op jit(solution)/shard_map/all_gather | solution.py:31
  9.0 131.7 %all-gather.5.cloned.1.call-start = ((), (), s32[]{:S(2)}) async-start(), calls=%async_computation.3 | async-start | bytes 3276800 | tf_op jit(solution)/shard_map/all_gather | solution.py:30
  10.7 218.7 %reduce-scatter.2.cloned.1.call-start = ((), (), s32[]{:S(2)}) async-start(), calls=%async_computation.2 | async-start | bytes 3276800 | tf_op jit(solution)/shard_map/reduce_scatter | solution.py:36
  84.1 0.8 copy-start.1
Sparse Core Ops, SparseCore 0:
  11.0 68.7 all-gather.2
  82.9 57.8 all-gather.4
  143.8 85.5 reduce-scatter.1
where the time goes:
time: 240 us; the launch traced here: 238 us
  waiting for transfers between devices  200 us (83%)
  matrix products  14.8 us (6%)
  between operations  13.8 us (6%)
  other arithmetic  4.97 us (2%)
  local copies, waits for them, and re-layouts  3.96 us (2%)
    reduce_scatter x1, waiting for transfers between devices, on_device(): lax.psum_scatter(contract_cols(hid_grad, w_in).astype(jnp.bfloat16), 'ten...  78.6 us
    all_gather x1, waiting for transfers between devices, on_device(): lax.all_gather(grad_bf, 'tensor', axis=0, tiled=True)  69.1 us
    all_gather x1, waiting for transfers between devices, on_device(): lax.all_gather(inputs_bf, 'tensor', axis=0, tiled=True)  52.2 us
    dot_general x2, matrix products, contract_rows(): lax.dot_general(left, right, (((0,), (0,)), ((), ())), preferred_element_...  6.99 us
  transfers between devices with their start and end apart: 3, of which 3 were waited for; matrix products, arithmetic and copies ran while one was open for 8% of the time, Pallas kernels for 0%

commit v1 on v0

v1 whole, which is shorter than its diff:
```python
import jax
import jax.numpy as jnp
from jax import lax
from jax.experimental import pallas as pl
from jax.experimental.pallas import tpu as pltpu
from jax.sharding import PartitionSpec as P

MESH = pl.DeviceIdType.MESH
CHIPS = 12
TENSOR = 24
ROWS = 32
HALF = 16
D = 2048
FF = 384
TILE = 256
F32 = jnp.float32
BF16 = jnp.bfloat16


def kernel(
    inputs_hbm, grad_hbm, pre_hbm, win_hbm, wout_hbm,
    ig_hbm, gwi_hbm, gwo_hbm,
    stage_x, stage_g, xall, gall, pre, act, hid, win, wout,
    pown, outbox, inbox, rsend, rrecv, igv, gwi, gwo,
    load_sem, store_sem,
    g_send, g_recv, gp_send, gp_recv,
    x_send, x_recv, xp_send, xp_recv,
    b_send, b_recv, r_send, r_recv,
):
    me = lax.axis_index("tensor")
    z = me // 2
    c = lax.rem(me, 2)
    peer = me + 1 - 2 * c
    right = lax.rem(me + 2, TENSOR)
    left = lax.rem(me + TENSOR - 2, TENSOR)

    barrier = pltpu.get_barrier_semaphore()
    for other in (left, right, peer):
        pl.semaphore_signal(barrier, inc=1, device_id={"tensor": other}, device_id_type=MESH)

    loads = [
        pltpu.make_async_copy(src, dst, load_sem.at[i])
        for i, (src, dst) in enumerate((
            (grad_hbm, stage_g), (inputs_hbm, stage_x), (wout_hbm, wout), (pre_hbm, pre), (win_hbm, win),
        ))
    ]
    for load in loads:
        load.start()

    def chip(offset):
        return lax.rem(z + offset + CHIPS, CHIPS)

    def ring(buf, sends, recvs, owner, way, step, half):
        part = buf.at[owner, pl.ds(half * HALF, HALF)]
        return pltpu.make_async_remote_copy(
            src_ref=part, dst_ref=part, send_sem=sends.at[way, step, half], recv_sem=recvs.at[way, step, half],
            device_id={"tensor": left if way else right}, device_id_type=MESH,
        )

    def across(buf, sends, recvs, owner, way, step, half):
        part = buf.at[owner, pl.ds(half * HALF, HALF)]
        return pltpu.make_async_remote_copy(
            src_ref=part, dst_ref=part, send_sem=sends.at[way, step, half], recv_sem=recvs.at[way, step, half],
            device_id={"tensor": peer}, device_id_type=MESH,
        )

    def source(way, step):
        return chip(step) if way else chip(-step)

    def relay(buf, ring_sems, peer_sems, step, half, way, last):
        owner = 2 * source(way, step) + c
        ring(buf, *ring_sems, owner, way, step, half).wait_recv()
        if last is None:
            ring(buf, *ring_sems, owner, way, step + 1, half).start()
        elif last is not True:
            @pl.when(last)
            def _():
                ring(buf, *ring_sems, owner, way, step + 1, half).start()
        across(buf, *peer_sems, owner, way, step, half).start()

    def from_peer(buf, peer_sems, step, half, way):
        owner = 2 * source(way, step) + 1 - c
        across(buf, *peer_sems, owner, way, step, half).wait_recv()

    def begin(buf, ring_sems, peer_sems):
        for half in (0, 1):
            for way in (0, 1):
                ring(buf, *ring_sems, me, way, 1, half).start()
        for half in (0, 1):
            across(buf, *peer_sems, me, 0, 0, half).start()

    g_ring, g_peer = (g_send, g_recv), (gp_send, gp_recv)
    x_ring, x_peer = (x_send, x_recv), (xp_send, xp_recv)

    def box(slot):
        return pltpu.make_async_remote_copy(
            src_ref=outbox.at[slot], dst_ref=inbox.at[slot], send_sem=b_send.at[slot], recv_sem=b_recv.at[slot],
            device_id={"tensor": peer}, device_id_type=MESH,
        )

    def compute(chips, slots):
        owners = []
        for d in chips:
            owners += [2 * d + c, 2 * d + 1 - c]
        lhs = jnp.concatenate([gall[o] for o in owners], axis=0)
        back = jnp.dot(lhs, wout[...], preferred_element_type=F32)
        rows_pre = jnp.concatenate([pre[o] for o in owners], axis=0)
        rows_hid = jnp.where(rows_pre > 0.0, back, 0.0).astype(BF16)
        for i, o in enumerate(owners):
            hid[o] = rows_hid[i * ROWS:(i + 1) * ROWS]

        @pl.loop(0, D // TILE)
        def _(n):
            cols = pl.ds(pl.multiple_of(n * TILE, TILE), TILE)
            part = lax.dot_general(
                rows_hid, win[cols, :], (((1,), (1,)), ((), ())), preferred_element_type=F32
            )
            for i, slot in enumerate(slots):
                pown[slot, :, cols] = part[2 * i * ROWS:(2 * i + 1) * ROWS]
                outbox[slot, :, cols] = part[(2 * i + 1) * ROWS:(2 * i + 2) * ROWS].astype(BF16)
        for slot in slots:
            box(slot).start()

    def slot_of(way, k):
        return k + 6 if way else k

    def rs(way, step):
        if step == 1:
            rows = pl.ds(way * HALF, HALF)
            src, dst = rsend.at[way, step, rows], rrecv.at[way, step, rows]
        else:
            src, dst = rsend.at[way, step], rrecv.at[way, step]
        return pltpu.make_async_remote_copy(
            src_ref=src, dst_ref=dst, send_sem=r_send.at[way, step], recv_sem=r_recv.at[way, step],
            device_id={"tensor": left if way else right}, device_id_type=MESH,
        )

    loads[0].wait()
    gall[me] = stage_g[...].astype(BF16)
    loads[1].wait()
    xall[me] = stage_x[...].astype(BF16)
    pl.semaphore_wait(barrier, 3)

    begin(gall, g_ring, g_peer)
    loads[2].wait()
    loads[3].wait()
    act[...] = jnp.maximum(pre[...], jnp.zeros_like(pre))
    loads[4].wait()
    for half in (0, 1):
        across(gall, *g_peer, 2 * z + 1 - c, 0, 0, half).wait_recv()
    compute([z], [0])

    def gather_step(s, carry):
        for half in (0, 1):
            for way in (0, 1):
                relay(gall, g_ring, g_peer, s, half, way, None if half == way else s < 5)

        @pl.when(s == 5)
        def _():
            begin(xall, x_ring, x_peer)

        @pl.when(s > 1)
        def _():
            for half in (0, 1):
                for way in (0, 1):
                    from_peer(gall, g_peer, s - 1, half, way)
            compute([chip(s - 1), chip(1 - s)], [s - 1, s + 5])
        return carry

    lax.fori_loop(1, 6, gather_step, 0)
    for way in (0, 1):
        relay(gall, g_ring, g_peer, 6, way, way, True)
    for half in (0, 1):
        for way in (0, 1):
            from_peer(gall, g_peer, 5, half, way)
    compute([chip(5), chip(-5)], [5, 11])
    for way in (0, 1):
        from_peer(gall, g_peer, 6, way, way)
    compute([chip(6)], [6])

    def weight_tile(buf, right_ref, out_ref, out_hbm, sem, n):
        cols = pl.ds(pl.multiple_of(n * TILE, TILE), TILE)
        lhs = buf[:, :, cols].reshape(TENSOR * ROWS, TILE)
        rhs = right_ref[...].reshape(TENSOR * ROWS, FF)
        total = lax.dot_general(lhs, rhs, (((0,), (0,)), ((), ())), preferred_element_type=F32)
        out_ref[cols, :] = total.astype(BF16)
        pltpu.make_async_copy(out_ref.at[cols, :], out_hbm.at[cols, :], sem.at[n]).start()

    for step in range(1, 7):
        k = 7 - step
        if step > 1:
            for way in (0, 1):
                rs(way, step - 1).wait_recv()
        if step == 1:
            box(6).wait_recv()
            for way in (0, 1):
                rows = pl.ds(way * HALF, HALF)
                rsend[way, step, rows] = (pown[6, rows] + inbox[6, rows].astype(F32)).astype(BF16)
        else:
            for way in (0, 1):
                slot = slot_of(way, k)
                box(slot).wait_recv()
                if step == 2:
                    rows, rest = pl.ds(way * HALF, HALF), pl.ds((1 - way) * HALF, HALF)
                    rsend[way, step, rows] = (
                        pown[slot, rows] + inbox[slot, rows].astype(F32) + rrecv[way, 1, rows].astype(F32)
                    ).astype(BF16)
                    rsend[way, step, rest] = (pown[slot, rest] + inbox[slot, rest].astype(F32)).astype(BF16)
                else:
                    rsend[way, step] = (
                        pown[slot] + inbox[slot].astype(F32) + rrecv[way, step - 1].astype(F32)
                    ).astype(BF16)
        for way in (0, 1):
            rs(way, step).start()
        for half in (0, 1):
            for way in (0, 1):
                if step < 6:
                    relay(xall, x_ring, x_peer, step, half, way, None if step < 5 or half == way else True)
                elif half == way:
                    relay(xall, x_ring, x_peer, step, half, way, True)
        if step < 5:
            @pl.loop(2 * (step - 1), 2 * step)
            def _(n):
                weight_tile(gall, act, gwo, gwo_hbm, store_sem.at[0], n)

    for half in (0, 1):
        across(xall, *x_peer, 2 * z + 1 - c, 0, 0, half).wait_recv()
    for s in range(1, 7):
        for half in (0, 1):
            for way in (0, 1):
                if s < 6 or half == way:
                    from_peer(xall, x_peer, s, half, way)

    @pl.loop(0, D // TILE)
    def _(n):
        weight_tile(xall, hid, gwi, gwi_hbm, store_sem.at[1], n)

    box(0).wait_recv()
    for way in (0, 1):
        rs(way, 6).wait_recv()
    igv[...] = pown[0] + inbox[0].astype(F32) + rrecv[0, 6].astype(F32) + rrecv[1, 6].astype(F32)
    store = pltpu.make_async_copy(igv, ig_hbm, load_sem.at[0])
    store.start()

    for buf, sends, peers in ((gall, g_ring, g_peer), (xall, x_ring, x_peer)):
        for half in (0, 1):
            across(buf, *peers, me, 0, 0, half).wait_send()
        for s in range(1, 7):
            for half in (0, 1):
                for way in (0, 1):
                    if s < 6 or half == way:
                        ring(buf, *sends, me, way, s, half).wait_send()
                        across(buf, *peers, me, way, s, half).wait_send()
    for slot in range(CHIPS):
        box(slot).wait_send()
    for step in range(1, 7):
        for way in (0, 1):
            rs(way, step).wait_send()

    @pl.loop(0, D // TILE)
    def _(n):
        cols = pl.ds(pl.multiple_of(n * TILE, TILE), TILE)
        pltpu.make_async_copy(gwo.at[cols, :], gwo_hbm.at[cols, :], store_sem.at[0, n]).wait()
        pltpu.make_async_copy(gwi.at[cols, :], gwi_hbm.at[cols, :], store_sem.at[1, n]).wait()
    store.wait()


def on_device(inputs, out_grad, pre_saved, w_in, w_out_t):
    dma = pltpu.SemaphoreType.DMA
    any_spec = pl.BlockSpec(memory_space=pl.ANY)
    return pl.pallas_call(
        kernel,
        out_shape=(
            jax.ShapeDtypeStruct((ROWS, D), F32),
            jax.ShapeDtypeStruct((D, FF), BF16),
            jax.ShapeDtypeStruct((D, FF), BF16),
        ),
        in_specs=[any_spec] * 5,
        out_specs=[any_spec] * 3,
        scratch_shapes=[
            pltpu.VMEM((ROWS, D), F32),
            pltpu.VMEM((ROWS, D), F32),
            pltpu.VMEM((TENSOR, ROWS, D), BF16),
            pltpu.VMEM((TENSOR, ROWS, D), BF16),
            pltpu.VMEM((TENSOR, ROWS, FF), BF16),
            pltpu.VMEM((TENSOR, ROWS, FF), BF16),
            pltpu.VMEM((TENSOR, ROWS, FF), BF16),
            pltpu.VMEM((D, FF), BF16),
            pltpu.VMEM((D, FF), BF16),
            pltpu.VMEM((CHIPS, ROWS, D), F32),
            pltpu.VMEM((CHIPS, ROWS, D), BF16),
            pltpu.VMEM((CHIPS, ROWS, D), BF16),
            pltpu.VMEM((2, 7, ROWS, D), BF16),
            pltpu.VMEM((2, 7, ROWS, D), BF16),
            pltpu.VMEM((ROWS, D), F32),
            pltpu.VMEM((D, FF), BF16),
            pltpu.VMEM((D, FF), BF16),
            dma((5,)), dma((2, D // TILE)),
            dma((2, 7, 2)), dma((2, 7, 2)), dma((2, 7, 2)), dma((2, 7, 2)),
            dma((2, 7, 2)), dma((2, 7, 2)), dma((2, 7, 2)), dma((2, 7, 2)),
            dma((CHIPS,)), dma((CHIPS,)), dma((2, 7)), dma((2, 7)),
        ],
        compiler_params=pltpu.CompilerParams(
            collective_id=0, has_side_effects=True, vmem_limit_bytes=60 * 1024 * 1024
        ),
        cost_estimate=pl.CostEstimate(flops=4_831_838_208, bytes_accessed=8_000_000, transcendentals=0),
        name="expert_backward",
    )(inputs, out_grad, pre_saved.reshape(TENSOR, ROWS, FF), w_in, w_out_t)


def solution(mesh):
    in_specs = (
        P(("dp", "tensor"), None),
        P(("dp", "tensor"), None),
        P("dp", "tensor"),
        P(None, "tensor"),
        P(None, "tensor"),
    )
    out_specs = (P(("dp", "tensor"), None), P("dp", "tensor"), P("dp", "tensor"))
    return jax.shard_map(
        on_device, mesh=mesh, in_specs=in_specs, out_specs=out_specs, check_vma=False
    )
```

time: 240 us -> 85.3 us (0.36)
  waiting for transfers between devices: 200 us -> 0 us
  Pallas kernels: 0 us -> 78.8 us
  matrix products: 14.8 us -> 0 us
  between operations: 13.8 us -> 0.64 us
  other arithmetic: 4.97 us -> 0 us
    all_gather x2 -> x0, waiting for transfers between devices: 121 us -> none  [the longest x1 69.1 us: on_device(): lax.all_gather(grad_bf, 'tensor', axis=0, tiled=True)]
    pallas_call x0 -> x1, Pallas kernels: none -> 78.8 us  [on_device(): pl.pallas_call(kernel, out_shape=(jax.ShapeDtypeStruct((ROWS, D), F32), j...]
    reduce_scatter x1 -> x0, waiting for transfers between devices: 78.6 us -> none  [on_device(): lax.psum_scatter(contract_cols(hid_grad, w_in).astype(jnp.bfloat16), 'ten...]
    dot_general x4 -> x0, matrix products: 14.8 us -> none  [the longest x2 6.99 us: contract_rows(): lax.dot_general(left, right, (((0,), (0,)), ((), ())), preferred_element_...]
    convert_element_type x3 -> x0, other arithmetic: 4.97 us -> none  [the longest x1 1.73 us: on_device(): grad_bf = out_grad.astype(jnp.bfloat16)]
    unnamed x6 -> x5, local copies, waits for them, and re-layouts: 3.96 us -> 5.64 us
  transfers between devices with their start and end apart: 3 -> 0, of which waited for: 3 -> 0; matrix products, arithmetic and copies ran while one was open for 8% -> 0% of each run, Pallas kernels for 0% -> 0%
where the time goes in v1:
time: 85.3 us; the launch traced here: 85.1 us
  Pallas kernels  78.8 us (92%)
  local copies, waits for them, and re-layouts  5.64 us (7%)
    pallas_call x1, Pallas kernels, on_device(): pl.pallas_call(kernel, out_shape=(jax.ShapeDtypeStruct((ROWS, D), F32), j...  78.8 us
    unnamed x5, local copies, waits for them, and re-layouts  5.64 us

profile of v1, /device:TPU:1, one launch (start us, length us, event | category | flops | bytes accessed | tf_op | source)
XLA Modules:
  0.0 85.1 jit_solution(10898314574480420305)
XLA Ops:
  0.6 78.8 %expert_backward.1 = (f32[32,2048]{1,0:T(8,128)}, bf16[2048,384]{1,0:T(8,128)(2,1)}, bf16[2048,384]{1,0:T(8,128)(2,1)}) custom-call(f32[32,2048]{1,0:T(8,128)} %inputs_hbm.1, f32[32,2048]{1,0:T(8,128)} %grad_hbm.1, bf16[24,32,384]{2,1,0:T(8,128)(2,1)} %bitcast.1, bf16[2048,384]{1,0:T(8,128)(2,1)} %win_hbm.1, bf16[2048,384]{1,0:T(8,128)(2,1)} %wout_hbm.1), custom_call_target="tpu_custom_call" | custom-call | flops 4831838208 | bytes 8000000 | tf_op jit(solution)/shard_map/expert_backward/pallas_call | solution.py:271
  79.5 1.7 %copy.11 = f32[32,2048]{1,0:T(8,128)} copy(f32[32,2048]{1,0:T(8,128)} %get-tuple-element.6) | data formatting | bytes 524288
  81.1 0.0 copy-start
  81.1 2.8 %copy.12 = bf16[2048,384]{1,0:T(8,128)(2,1)} copy(bf16[2048,384]{1,0:T(8,128)(2,1)} %get-tuple-element.7) | data formatting | bytes 3145728
  84.0 0.0 copy-done
  84.0 1.1 %copy.13 = bf16[2048,384]{1,0:T(8,128)(2,1)} copy(bf16[2048,384]{1,0:T(8,128)(2,1)S(1)} %copy-done) | data formatting | bytes 3145728
Async XLA Ops:
  81.1 2.8 %copy-start = (bf16[2048,384]{1,0:T(8,128)(2,1)S(1)}, bf16[2048,384]{1,0:T(8,128)(2,1)}, u32[]{:S(2)}) copy-start(bf16[2048,384]{1,0:T(8,128)(2,1)} %get-tuple-element.8) | copy-start | bytes 4718596

commit v2 on v0

v2 whole, which is shorter than its diff:
```python
import jax
import jax.numpy as jnp
from jax import lax
from jax.experimental import pallas as pl
from jax.experimental.pallas import tpu as pltpu
from jax.sharding import PartitionSpec as P

MESH = pl.DeviceIdType.MESH
CHIPS = 12
TENSOR = 24
ROWS = 32
HALF = 16
D = 2048
COLS = 1024
FF = 384
TILE = 512
TILES = D // TILE
GRAIN = 256
GRAINS = D // GRAIN
F32 = jnp.float32
BF16 = jnp.bfloat16

LAG = 10
FAR = 20
NEAR = 28


def pieces_of(s):
    return range(4) if s == 6 else range(8)


def message_order():
    gather = [(s, j) for s in range(1, 7) for j in pieces_of(s)]
    reduce = [(1, j) for j in range(4)] + [(2, j) for j in (4, 5, 6, 7, 0, 1, 2, 3)]
    reduce += [(s, j) for s in range(3, 7) for j in (4, 5, 6, 7, 0, 1, 2, 3)]
    todo = {"g": list(gather), "r": reduce, "x": list(gather)}
    slot = {}
    t = 0

    def ready(kind, s, j):
        if kind == "r" and s == 1:
            need, lag = [("g", 6, i) for i in range(4)], FAR
        elif kind == "r" and s == 2 and j > 3:
            need, lag = [("g", 5, i) for i in range(8)], NEAR
        elif s == 1:
            return True
        else:
            need, lag = [(kind, s - 1, j)], LAG
        if kind == "r" and s == 6 and todo["x"]:
            return False
        return all(m in slot and slot[m] + lag <= t for m in need)

    while any(todo.values()):
        for kind in "grx":
            if todo[kind] and ready(kind, *todo[kind][0]):
                slot[(kind,) + todo[kind].pop(0)] = t
                break
        t += 1
    return slot


def kernel(
    inputs_hbm, grad_hbm, pre_hbm, win_hbm, wout_hbm,
    igv, gwi, gwo,
    stage_x, stage_g, xall, gall, pre, act, hid, win, wout,
    pown, outbox, inbox, rsend, rrecv, rlast, acc,
    load_sem,
    g_send, g_recv, gp_send, gp_recv,
    x_send, x_recv, xp_send, xp_recv,
    b_send, b_recv, r_send, r_recv, l_send, l_recv,
):
    me = lax.axis_index("tensor")
    z = me // 2
    c = lax.rem(me, 2)
    sign = 1 - 2 * c
    peer = me + sign
    after = lax.rem(me + 2 * sign + TENSOR, TENSOR)
    before = lax.rem(me - 2 * sign + TENSOR, TENSOR)

    barrier = pltpu.get_barrier_semaphore()
    for other in (after, before, peer):
        pl.semaphore_signal(barrier, inc=1, device_id={"tensor": other}, device_id_type=MESH)

    loads = [
        pltpu.make_async_copy(src, dst, load_sem.at[i])
        for i, (src, dst) in enumerate((
            (grad_hbm, stage_g), (inputs_hbm, stage_x), (wout_hbm, wout), (pre_hbm, pre), (win_hbm, win),
        ))
    ]
    for load in loads:
        load.start()

    def chip(offset):
        return lax.rem(z + offset * sign + CHIPS, CHIPS)

    def owner_of(d, j):
        return 2 * d + (c if j < 4 else 1 - c)

    def part(j):
        return pl.ds(j % 4 // 2 * HALF, HALF), pl.ds(j % 2 * COLS, COLS)

    def part64(j):
        return pl.ds(j // 2 * HALF, HALF), pl.ds(j % 2 * COLS, COLS)

    bufs = {"g": gall, "x": xall}
    ring_sems = {"g": (g_send, g_recv), "x": (x_send, x_recv), "r": (r_send, r_recv)}
    peer_sems = {"g": (gp_send, gp_recv), "x": (xp_send, xp_recv)}

    def ring(kind, s, j, d):
        sends, recvs = ring_sems[kind]
        if kind == "r":
            rows, cols = part64(j)
            src, dst = rsend.at[s, rows, cols], rrecv.at[s, rows, cols]
        else:
            rows, cols = part(j)
            src = dst = bufs[kind].at[owner_of(d, j), rows, cols]
        return pltpu.make_async_remote_copy(
            src_ref=src, dst_ref=dst, send_sem=sends.at[s, j], recv_sem=recvs.at[s, j],
            device_id={"tensor": after}, device_id_type=MESH,
        )

    def to_peer(src, dst, send, recv):
        return pltpu.make_async_remote_copy(
            src_ref=src, dst_ref=dst, send_sem=send, recv_sem=recv, device_id={"tensor": peer}, device_id_type=MESH,
        )

    def across(kind, s, j, owner):
        rows, cols = part(j)
        piece = bufs[kind].at[owner, rows, cols]
        sends, recvs = peer_sems[kind]
        return to_peer(piece, piece, sends.at[s, j], recvs.at[s, j])

    def across_own(kind, owner):
        piece = bufs[kind].at[owner]
        sends, recvs = peer_sems[kind]
        return to_peer(piece, piece, sends.at[0, 0], recvs.at[0, 0])

    def from_peer(kind, s):
        for j in pieces_of(s):
            across(kind, s, j, 2 * chip(s) + (1 - c if j < 4 else c)).wait_recv()

    def box(k):
        rows = pl.ds(0, ROWS if k in (0, 6) else 2 * ROWS)
        return to_peer(outbox.at[k, rows], inbox.at[k, rows], b_send.at[k], b_recv.at[k])

    def handover():
        rows = pl.ds(ROWS, ROWS)
        return to_peer(rrecv.at[6, rows], rlast, l_send, l_recv)

    def rows_of(k):
        near, far = chip(k), chip(-k)
        if k in (0, 6):
            return [2 * near + c, 2 * near + 1 - c]
        return [2 * near + c, 2 * near + 1 - c, 2 * far + 1 - c, 2 * far + c]

    def hidden(k):
        owners = rows_of(k)
        lhs = jnp.concatenate([gall[o] for o in owners], axis=0)
        back = jnp.dot(lhs, wout[...], preferred_element_type=F32)
        rows_pre = jnp.concatenate([pre[o] for o in owners], axis=0)
        rows_hid = jnp.where(rows_pre > 0.0, back, 0.0).astype(BF16)
        for i, o in enumerate(owners):
            hid[o] = rows_hid[i * ROWS:(i + 1) * ROWS]

    def share(k, n):
        owners = rows_of(k)
        rows_hid = jnp.concatenate([hid[o] for o in owners], axis=0)
        half = len(owners) // 2 * ROWS
        cols = pl.ds(n * TILE, TILE)
        sums = lax.dot_general(rows_hid, win[cols, :], (((1,), (1,)), ((), ())), preferred_element_type=F32)
        pown[k, :half, cols] = sums[:half]
        outbox[k, :half, cols] = sums[half:].astype(BF16)
        if n == TILES - 1:
            box(k).start()

    def own_rows():
        for load in loads[2:]:
            load.wait()
        hidden(0)

    def near_rows(k):
        from_peer("g", k)
        hidden(k)

    def far_rows():
        from_peer("g", 6)
        hidden(6)
        for n in range(TILES):
            share(6, n)

    def activations():
        act[...] = jnp.maximum(pre[...], jnp.zeros_like(pre))

    def out_tile(n):
        cols = pl.ds(n * GRAIN, GRAIN)
        lhs = gall[:, :, cols].reshape(TENSOR * ROWS, GRAIN)
        rhs = act[...].reshape(TENSOR * ROWS, FF)
        total = lax.dot_general(rhs, lhs, (((0,), (0,)), ((), ())), preferred_element_type=F32)
        gwo[cols, :] = total.T.astype(BF16)

    early = [0, 1, -1, 2, -2, 3, -3, 4]
    late = [-4, 5, -5, 6]

    def in_tile(n, offsets):
        cols = pl.ds(n * GRAIN, GRAIN)
        owners = [o for k in offsets for o in (2 * chip(k) + c, 2 * chip(k) + 1 - c)]
        lhs = jnp.concatenate([xall[o, :, cols] for o in owners], axis=0)
        rhs = jnp.concatenate([hid[o] for o in owners], axis=0)
        total = lax.dot_general(rhs, lhs, (((0,), (0,)), ((), ())), preferred_element_type=F32)
        if offsets is early:
            acc[:, cols] = total
        else:
            gwi[cols, :] = (acc[:, cols] + total).T.astype(BF16)

    def in_tile_early(n):
        in_tile(n, early)

    def in_tile_late(n):
        in_tile(n, late)

    def early_inputs():
        for k in range(1, 5):
            from_peer("x", k)

    def late_inputs():
        for k in (5, 6):
            from_peer("x", k)

    slot = message_order()
    pieces = {}

    def at(when, piece, *args):
        pieces.setdefault(int(when), []).append((piece, args))

    def at_each(when, count, step, piece, *args):
        for n in range(count):
            at(when + n * step, piece, *args, n)

    def arrival(kind, s):
        return max(slot[(kind, s, j)] for j in pieces_of(s)) + LAG

    at(6, own_rows)
    at_each(8, TILES, 1, share, 0)
    at(13, activations)
    for k in range(1, 5):
        at(arrival("g", k) + 3, near_rows, k)
        at_each(arrival("g", k) + 4, TILES, 1, share, k)
    far = arrival("g", 6) + 2
    at(far, far_rows)
    at(far + 1, near_rows, 5)
    at_each(far + 2, TILES, 1, share, 5)
    at_each(far + 10, GRAINS, 2, out_tile)
    begin = max(arrival("x", 4) + 4, far + 10 + 2 * GRAINS)
    at(begin, early_inputs)
    at_each(begin, GRAINS, 1.5, in_tile_early)
    end = max(arrival("x", 6) + 4, begin + int(GRAINS * 1.5))
    at(end, late_inputs)
    at_each(end, GRAINS, 1, in_tile_late)

    boxed = set()

    def mailed(k):
        if k not in boxed:
            boxed.add(k)
            box(k).wait_recv()

    loads[0].wait()
    gall[me] = stage_g[...].astype(BF16)
    pl.semaphore_wait(barrier, 3)
    across_own("g", me).start()

    at_slot = {t: message for message, t in slot.items()}
    last = max(slot.values())
    for t in range(max(last + LAG, *pieces) + 1):
        came = at_slot.get(t - LAG)
        if came is not None:
            kind, s, j = came
            d = chip(-s)
            ring(kind, s, j, d).wait_recv()
            if kind != "r":
                across(kind, s, j, owner_of(d, j)).start()
            elif (s, j) == (6, 7):
                handover().start()
        goes = at_slot.get(t)
        if goes is not None:
            kind, s, j = goes
            if goes == ("x", 1, 0):
                loads[1].wait()
                xall[me] = stage_x[...].astype(BF16)
                across_own("x", me).start()
            if goes in (("g", 1, 4), ("x", 1, 4)):
                across_own(kind, peer).wait_recv()
            if kind == "r":
                k = 7 - s
                mailed(k)
                rows, cols = part64(j)
                total = pown[k, rows, cols] + inbox[k, rows, cols].astype(F32)
                if s > 2 or s == 2 and j < 4:
                    total += rrecv[s - 1, rows, cols].astype(F32)
                rsend[s, rows, cols] = total.astype(BF16)
            ring(kind, s, j, chip(1 - s)).start()
        for piece, args in pieces.get(t, ()):
            piece(*args)

    mailed(0)
    igv[...] = pown[0, :ROWS] + inbox[0, :ROWS].astype(F32) + rrecv[6, :ROWS].astype(F32)
    handover().wait_recv()
    igv[...] += rlast[...].astype(F32)

    for kind in "gx":
        across_own(kind, me).wait_send()
    for kind in "gxr":
        for s in range(1, 7):
            for j in range(8) if kind == "r" and s > 1 else range(4) if kind == "r" else pieces_of(s):
                ring(kind, s, j, z).wait_send()
                if kind != "r":
                    across(kind, s, j, owner_of(z, j)).wait_send()
    for k in range(7):
        box(k).wait_send()
    handover().wait_send()


def write_out(ig, gwi, gwo, ig_hbm, gwi_hbm, gwo_hbm, sem):
    copies = [
        pltpu.make_async_copy(src, dst, sem.at[i])
        for i, (src, dst) in enumerate(((gwi, gwi_hbm), (gwo, gwo_hbm), (ig, ig_hbm)))
    ]
    for copy in copies:
        copy.start()
    for copy in copies:
        copy.wait()


def on_device(inputs, out_grad, pre_saved, w_in, w_out_t):
    dma = pltpu.SemaphoreType.DMA
    any_spec = pl.BlockSpec(memory_space=pl.ANY)
    vmem_spec = pl.BlockSpec(memory_space=pltpu.VMEM)
    shapes = (((ROWS, D), F32), ((D, FF), BF16), ((D, FF), BF16))
    results = pl.pallas_call(
        kernel,
        out_shape=tuple(pltpu.VMEM(*shape) for shape in shapes),
        in_specs=[pl.BlockSpec(memory_space=pltpu.HBM)] * 5,
        out_specs=(vmem_spec,) * 3,
        scratch_shapes=[
            pltpu.VMEM((ROWS, D), F32),
            pltpu.VMEM((ROWS, D), F32),
            pltpu.VMEM((TENSOR, ROWS, D), BF16),
            pltpu.VMEM((TENSOR, ROWS, D), BF16),
            pltpu.VMEM((TENSOR, ROWS, FF), BF16),
            pltpu.VMEM((TENSOR, ROWS, FF), BF16),
            pltpu.VMEM((TENSOR, ROWS, FF), BF16),
            pltpu.VMEM((D, FF), BF16),
            pltpu.VMEM((D, FF), BF16),
            pltpu.VMEM((7, 2 * ROWS, D), F32),
            pltpu.VMEM((7, 2 * ROWS, D), BF16),
            pltpu.VMEM((7, 2 * ROWS, D), BF16),
            pltpu.VMEM((7, 2 * ROWS, D), BF16),
            pltpu.VMEM((7, 2 * ROWS, D), BF16),
            pltpu.VMEM((ROWS, D), BF16),
            pltpu.VMEM((FF, D), F32),
            dma((5,)),
            dma((7, 8)), dma((7, 8)), dma((7, 8)), dma((7, 8)),
            dma((7, 8)), dma((7, 8)), dma((7, 8)), dma((7, 8)),
            dma((7,)), dma((7,)), dma((7, 8)), dma((7, 8)), dma, dma,
        ],
        compiler_params=pltpu.CompilerParams(
            collective_id=0, has_side_effects=True, vmem_limit_bytes=60 * 1024 * 1024
        ),
        cost_estimate=pl.CostEstimate(flops=4_831_838_208, bytes_accessed=8_000_000, transcendentals=0),
        name="expert_backward",
    )(inputs, out_grad, pre_saved.reshape(TENSOR, ROWS, FF), w_in, w_out_t)
    return pl.pallas_call(
        write_out,
        out_shape=tuple(jax.ShapeDtypeStruct(*shape) for shape in shapes),
        in_specs=[any_spec] * 3,
        out_specs=(any_spec,) * 3,
        scratch_shapes=[dma((3,))],
        compiler_params=pltpu.CompilerParams(vmem_limit_bytes=2 * 1024 * 1024),
        name="write_out",
    )(*results)


def solution(mesh):
    in_specs = (
        P(("dp", "tensor"), None),
        P(("dp", "tensor"), None),
        P("dp", "tensor"),
        P(None, "tensor"),
        P(None, "tensor"),
    )
    out_specs = (P(("dp", "tensor"), None), P("dp", "tensor"), P("dp", "tensor"))
    return jax.shard_map(
        on_device, mesh=mesh, in_specs=in_specs, out_specs=out_specs, check_vma=False
    )
```

time: 240 us -> 73.7 us (0.31)
  waiting for transfers between devices: 200 us -> 0 us
  Pallas kernels: 0 us -> 72.8 us
  matrix products: 14.8 us -> 0 us
  between operations: 13.8 us -> 0.8 us
  other arithmetic: 4.97 us -> 0 us
  local copies, waits for them, and re-layouts: 3.96 us -> 0 us
    all_gather x2 -> x0, waiting for transfers between devices: 121 us -> none  [the longest x1 69.1 us: on_device(): lax.all_gather(grad_bf, 'tensor', axis=0, tiled=True)]
    reduce_scatter x1 -> x0, waiting for transfers between devices: 78.6 us -> none  [on_device(): lax.psum_scatter(contract_cols(hid_grad, w_in).astype(jnp.bfloat16), 'ten...]
    pallas_call x0 -> x2, Pallas kernels: none -> 72.8 us  [the longest x1 71 us: on_device(): pl.pallas_call(kernel, out_shape=tuple((pltpu.VMEM(*shape) for shape in s...]
    dot_general x4 -> x0, matrix products: 14.8 us -> none  [the longest x2 6.99 us: contract_rows(): lax.dot_general(left, right, (((0,), (0,)), ((), ())), preferred_element_...]
    convert_element_type x3 -> x0, other arithmetic: 4.97 us -> none  [the longest x1 1.73 us: on_device(): grad_bf = out_grad.astype(jnp.bfloat16)]
    unnamed x6 -> x0, local copies, waits for them, and re-layouts: 3.96 us -> none
  transfers between devices with their start and end apart: 3 -> 0, of which waited for: 3 -> 0; matrix products, arithmetic and copies ran while one was open for 8% -> 0% of each run, Pallas kernels for 0% -> 0%
where the time goes in v2:
time: 73.7 us; the launch traced here: 73.6 us
  Pallas kernels  72.8 us (99%)
  between operations  0.8 us (1%)
    pallas_call x1, Pallas kernels, on_device(): pl.pallas_call(kernel, out_shape=tuple((pltpu.VMEM(*shape) for shape in s...  71 us
    pallas_call x1, Pallas kernels, on_device(): pl.pallas_call(write_out, out_shape=tuple((jax.ShapeDtypeStruct(*shape) f...  1.77 us

profile of v2, /device:TPU:1, one launch (start us, length us, event | category | flops | bytes accessed | tf_op | source)
XLA Modules:
  0.0 73.6 jit_solution(16020333881870251356)
XLA Ops:
  0.6 71.0 %expert_backward.1 = (f32[32,2048]{1,0:T(8,128)S(1)}, bf16[2048,384]{1,0:T(8,128)(2,1)S(1)}, bf16[2048,384]{1,0:T(8,128)(2,1)S(1)}) custom-call(f32[32,2048]{1,0:T(8,128)} %inputs_hbm.1, f32[32,2048]{1,0:T(8,128)} %grad_hbm.1, bf16[24,32,384]{2,1,0:T(8,128)(2,1)} %bitcast.1, bf16[2048,384]{1,0:T(8,128)(2,1)} %win_hbm.1, bf16[2048,384]{1,0:T(8,128)(2,1)} %wout_hbm.1), custom_call_target="tpu_custom_call" | custom-call | flops 4831838208 | bytes 8000000 | tf_op jit(solution)/shard_map/expert_backward/pallas_call | solution.py:339
  71.6 1.8 %write_out.1 = (f32[32,2048]{1,0:T(8,128)}, bf16[2048,384]{1,0:T(8,128)(2,1)}, bf16[2048,384]{1,0:T(8,128)(2,1)}) custom-call(f32[32,2048]{1,0:T(8,128)S(1)} %get-tuple-element.6.ig, bf16[2048,384]{1,0:T(8,128)(2,1)S(1)} %get-tuple-element.7.gwi, bf16[2048,384]{1,0:T(8,128)(2,1)S(1)} %get-tuple-element.8.gwo), custom_call_target="tpu_custom_call" | custom-call | tf_op jit(solution)/shard_map/write_out/pallas_call | solution.py:372

commit v3 on v2

--- a/solution.py
+++ b/solution.py
@@ -22,7 +22,7 @@
 
 LAG = 10
 FAR = 20
-NEAR = 28
+NEAR = 30
 
 
 def pieces_of(s):
@@ -43,7 +43,7 @@
         elif kind == "r" and s == 2 and j > 3:
             need, lag = [("g", 5, i) for i in range(8)], NEAR
         elif s == 1:
-            return True
+            return kind == "x" or j < 4 or t > 5
         else:
             need, lag = [(kind, s - 1, j)], LAG
         if kind == "r" and s == 6 and todo["x"]:
@@ -87,8 +87,7 @@
             (grad_hbm, stage_g), (inputs_hbm, stage_x), (wout_hbm, wout), (pre_hbm, pre), (win_hbm, win),
         ))
     ]
-    for load in loads:
-        load.start()
+    loads[0].start()
 
     def chip(offset):
         return lax.rem(z + offset * sign + CHIPS, CHIPS)
@@ -185,8 +184,6 @@
     def far_rows():
         from_peer("g", 6)
         hidden(6)
-        for n in range(TILES):
-            share(6, n)
 
     def activations():
         act[...] = jnp.maximum(pre[...], jnp.zeros_like(pre))
@@ -247,15 +244,16 @@
         at_each(arrival("g", k) + 4, TILES, 1, share, k)
     far = arrival("g", 6) + 2
     at(far, far_rows)
-    at(far + 1, near_rows, 5)
-    at_each(far + 2, TILES, 1, share, 5)
-    at_each(far + 10, GRAINS, 2, out_tile)
-    begin = max(arrival("x", 4) + 4, far + 10 + 2 * GRAINS)
+    at_each(far + 1, TILES, 1, share, 6)
+    at(far + 5, near_rows, 5)
+    at_each(far + 6, TILES, 1, share, 5)
+    at_each(far + 12, GRAINS, 2, out_tile)
+    begin = max(arrival("x", 4) + 4, far + 12 + 2 * GRAINS)
     at(begin, early_inputs)
     at_each(begin, GRAINS, 1.5, in_tile_early)
     end = max(arrival("x", 6) + 4, begin + int(GRAINS * 1.5))
     at(end, late_inputs)
-    at_each(end, GRAINS, 1, in_tile_late)
+    at_each(end, GRAINS, 0.5, in_tile_late)
 
     boxed = set()
 
@@ -265,6 +263,8 @@
             box(k).wait_recv()
 
     loads[0].wait()
+    for load in loads[1:]:
+        load.start()
     gall[me] = stage_g[...].astype(BF16)
     pl.semaphore_wait(barrier, 3)
     across_own("g", me).start()

time: 73.7 us -> 72 us (0.977)
  Pallas kernels: 72.8 us -> 71.2 us
    pallas_call x1, Pallas kernels: 71 us -> 69.5 us  [on_device(): pl.pallas_call(kernel, out_shape=tuple((pltpu.VMEM(*shape) for shape in s...]
where the time goes in v3:
time: 72 us; the launch traced here: 71.9 us
  Pallas kernels  71.2 us (99%)
    pallas_call x1, Pallas kernels, on_device(): pl.pallas_call(kernel, out_shape=tuple((pltpu.VMEM(*shape) for shape in s...  69.5 us
    pallas_call x1, Pallas kernels, on_device(): pl.pallas_call(write_out, out_shape=tuple((jax.ShapeDtypeStruct(*shape) f...  1.77 us

profile of v3, /device:TPU:1, one launch (start us, length us, event | category | flops | bytes accessed | tf_op | source)
XLA Modules:
  0.0 71.9 jit_solution(8577203481553990992)
XLA Ops:
  0.6 69.5 %expert_backward.1 = (f32[32,2048]{1,0:T(8,128)S(1)}, bf16[2048,384]{1,0:T(8,128)(2,1)S(1)}, bf16[2048,384]{1,0:T(8,128)(2,1)S(1)}) custom-call(f32[32,2048]{1,0:T(8,128)} %inputs_hbm.1, f32[32,2048]{1,0:T(8,128)} %grad_hbm.1, bf16[24,32,384]{2,1,0:T(8,128)(2,1)} %bitcast.1, bf16[2048,384]{1,0:T(8,128)(2,1)} %win_hbm.1, bf16[2048,384]{1,0:T(8,128)(2,1)} %wout_hbm.1), custom_call_target="tpu_custom_call" | custom-call | flops 4831838208 | bytes 8000000 | tf_op jit(solution)/shard_map/expert_backward/pallas_call | solution.py:339
  70.1 1.8 %write_out.1 = (f32[32,2048]{1,0:T(8,128)}, bf16[2048,384]{1,0:T(8,128)(2,1)}, bf16[2048,384]{1,0:T(8,128)(2,1)}) custom-call(f32[32,2048]{1,0:T(8,128)S(1)} %get-tuple-element.6.ig, bf16[2048,384]{1,0:T(8,128)(2,1)S(1)} %get-tuple-element.7.gwi, bf16[2048,384]{1,0:T(8,128)(2,1)S(1)} %get-tuple-element.8.gwo), custom_call_target="tpu_custom_call" | custom-call | tf_op jit(solution)/shard_map/write_out/pallas_call | solution.py:372

commit v4 on v3

--- a/solution.py
+++ b/solution.py
@@ -87,7 +87,12 @@
             (grad_hbm, stage_g), (inputs_hbm, stage_x), (wout_hbm, wout), (pre_hbm, pre), (win_hbm, win),
         ))
     ]
-    loads[0].start()
+    firsts = [
+        pltpu.make_async_copy(grad_hbm.at[rows, :], stage_g.at[rows, :], load_sem.at[sem])
+        for sem, rows in ((0, pl.ds(0, HALF)), (5, pl.ds(HALF, HALF)))
+    ]
+    for load in firsts:
+        load.start()
 
     def chip(offset):
         return lax.rem(z + offset * sign + CHIPS, CHIPS)
@@ -262,7 +267,8 @@
             boxed.add(k)
             box(k).wait_recv()
 
-    loads[0].wait()
+    for load in firsts:
+        load.wait()
     for load in loads[1:]:
         load.start()
     gall[me] = stage_g[...].astype(BF16)
@@ -321,10 +327,11 @@
 
 
 def write_out(ig, gwi, gwo, ig_hbm, gwi_hbm, gwo_hbm, sem):
-    copies = [
-        pltpu.make_async_copy(src, dst, sem.at[i])
-        for i, (src, dst) in enumerate(((gwi, gwi_hbm), (gwo, gwo_hbm), (ig, ig_hbm)))
-    ]
+    pairs = [(ig, ig_hbm)]
+    for n in range(TILES):
+        rows = pl.ds(n * TILE, TILE)
+        pairs += [(gwi.at[rows, :], gwi_hbm.at[rows, :]), (gwo.at[rows, :], gwo_hbm.at[rows, :])]
+    copies = [pltpu.make_async_copy(src, dst, sem.at[i]) for i, (src, dst) in enumerate(pairs)]
     for copy in copies:
         copy.start()
     for copy in copies:
@@ -358,7 +365,7 @@
             pltpu.VMEM((7, 2 * ROWS, D), BF16),
             pltpu.VMEM((ROWS, D), BF16),
             pltpu.VMEM((FF, D), F32),
-            dma((5,)),
+            dma((6,)),
             dma((7, 8)), dma((7, 8)), dma((7, 8)), dma((7, 8)),
             dma((7, 8)), dma((7, 8)), dma((7, 8)), dma((7, 8)),
             dma((7,)), dma((7,)), dma((7, 8)), dma((7, 8)), dma, dma,
@@ -374,7 +381,7 @@
         out_shape=tuple(jax.ShapeDtypeStruct(*shape) for shape in shapes),
         in_specs=[any_spec] * 3,
         out_specs=(any_spec,) * 3,
-        scratch_shapes=[dma((3,))],
+        scratch_shapes=[dma((2 * TILES + 1,))],
         compiler_params=pltpu.CompilerParams(vmem_limit_bytes=2 * 1024 * 1024),
         name="write_out",
     )(*results)

time: 72 us -> 72.1 us (level)
  no operation moved by 1% of the time
where the time goes in v4:
time: 72.1 us; the launch traced here: 71.9 us
  Pallas kernels  71.3 us (99%)
    pallas_call x1, Pallas kernels, on_device(): pl.pallas_call(kernel, out_shape=tuple((pltpu.VMEM(*shape) for shape in s...  69.5 us
    pallas_call x1, Pallas kernels, on_device(): pl.pallas_call(write_out, out_shape=tuple((jax.ShapeDtypeStruct(*shape) f...  1.82 us

profile of v4, /device:TPU:1, one launch (start us, length us, event | category | flops | bytes accessed | tf_op | source)
XLA Modules:
  0.0 71.9 jit_solution(3477706900545730694)
XLA Ops:
  0.6 69.5 %expert_backward.1 = (f32[32,2048]{1,0:T(8,128)S(1)}, bf16[2048,384]{1,0:T(8,128)(2,1)S(1)}, bf16[2048,384]{1,0:T(8,128)(2,1)S(1)}) custom-call(f32[32,2048]{1,0:T(8,128)} %inputs_hbm.1, f32[32,2048]{1,0:T(8,128)} %grad_hbm.1, bf16[24,32,384]{2,1,0:T(8,128)(2,1)} %bitcast.1, bf16[2048,384]{1,0:T(8,128)(2,1)} %win_hbm.1, bf16[2048,384]{1,0:T(8,128)(2,1)} %wout_hbm.1), custom_call_target="tpu_custom_call" | custom-call | flops 4831838208 | bytes 8000000 | tf_op jit(solution)/shard_map/expert_backward/pallas_call | solution.py:346
  70.1 1.8 %write_out.1 = (f32[32,2048]{1,0:T(8,128)}, bf16[2048,384]{1,0:T(8,128)(2,1)}, bf16[2048,384]{1,0:T(8,128)(2,1)}) custom-call(f32[32,2048]{1,0:T(8,128)S(1)} %get-tuple-element.6.ig, bf16[2048,384]{1,0:T(8,128)(2,1)S(1)} %get-tuple-element.7.gwi, bf16[2048,384]{1,0:T(8,128)(2,1)S(1)} %get-tuple-element.8.gwo), custom_call_target="tpu_custom_call" | custom-call | tf_op jit(solution)/shard_map/write_out/pallas_call | solution.py:379
